TPU v7x, 32 devices: a whole 2x2x4 slice. The times are simulated.
32 devices in a mesh: dp: 4 (over y, x), ctx: 2 (over core), mp: 4 (over z).
Axes of the slice: x: 2, y: 2, z: 4, core: 2. Of those that a mesh axis runs over, the one named last changes fastest.
Arguments:
- inputs: bfloat16 [12, 1024, 1536], P('dp', ('ctx', 'mp')), may hold values from -6 to 6
- w_query: bfloat16 [1536, 1536], P(('dp', 'ctx'), 'mp'), may hold values from -0.21875 to 0.21875
- w_key: bfloat16 [1536, 1536], P(('dp', 'ctx'), 'mp'), may hold values from -0.21875 to 0.21875
- w_value: bfloat16 [1536, 1536], P(('dp', 'ctx'), 'mp'), may hold values from -0.15625 to 0.15625
- w_out: bfloat16 [1536, 1536], P('mp', ('dp', 'ctx')), may hold values from -0.875 to 0.875
- w_up: bfloat16 [1536, 8, 768], P(('dp', 'ctx'), None, 'mp'), may hold values from -0.15625 to 0.15625
- w_down: bfloat16 [8, 768, 1536], P(None, 'mp', ('dp', 'ctx')), may hold values from -0.15625 to 0.15625
- gain_attn: bfloat16 [1536], P(('dp', 'ctx')), may hold values from 0.099609375 to 1.8984375
- gain_ffn: bfloat16 [1536], P(('dp', 'ctx')), may hold values from 0.099609375 to 1.8984375
- cotangent: bfloat16 [12, 1024, 1536], P('dp', ('ctx', 'mp')), may hold values from -6 to 6
Outputs:
- outputs: bfloat16 [12, 1024, 1536], P('dp', ('ctx', 'mp'))
- input_grads: float32 [12, 1024, 1536], P('dp', ('ctx', 'mp'))
- grad_query: float32 [1536, 1536], P(('dp', 'ctx'), 'mp')
- grad_key: float32 [1536, 1536], P(('dp', 'ctx'), 'mp')
- grad_value: float32 [1536, 1536], P(('dp', 'ctx'), 'mp')
- grad_out: float32 [1536, 1536], P('mp', ('dp', 'ctx'))
- grad_up: float32 [1536, 8, 768], P(('dp', 'ctx'), None, 'mp')
- grad_down: float32 [8, 768, 1536], P(None, 'mp', ('dp', 'ctx'))
- grad_gain_attn: float32 [1536], P(('dp', 'ctx'))
- grad_gain_ffn: float32 [1536], P(('dp', 'ctx'))
All inputs are finite; a program needn't handle non-finite values.
Results may differ from a plain program's by a relative error of at most 0.015.
Values may be sent and summed in bfloat16 or wider, within the bound.
No kernel may reach another device: no remote copies, remote signals or barrier semaphores. Data moves between devices by JAX's collectives and lax.ppermute only.
A program may use at most 256 MiB of HBM per device.

v0:
```python
import jax
import jax.numpy as jnp
from jax import lax
from jax.sharding import PartitionSpec as P

HEAD = 128
EPSILON = 1e-06
NEGATIVE = -1e30


def from_behind(shard, axis, by):
    devices = lax.axis_size(axis)
    pairs = [(i, i + by) for i in range(devices) if 0 <= i + by < devices]
    return lax.ppermute(shard, axis, pairs)


def normalize(values, gain_vec):
    inv_rms = lax.rsqrt(jnp.mean(values * values, axis=-1, keepdims=True) + EPSILON)
    return values * inv_rms * gain_vec


def unit_rows(values):
    return values * lax.rsqrt(jnp.mean(values * values, axis=-1, keepdims=True) + EPSILON)


def norm_back(values, gain_vec, grad_normed):
    inv_rms = lax.rsqrt(jnp.mean(values * values, axis=-1, keepdims=True) + EPSILON)
    weighted = grad_normed * gain_vec
    return inv_rms * weighted - values * (inv_rms * inv_rms * inv_rms) * jnp.mean(
        weighted * values, axis=-1, keepdims=True
    )


def rotation(positions, head_size):
    half_size = head_size // 2
    frequency = 10000.0 ** (-jnp.arange(half_size, dtype=jnp.float32) / half_size)
    angles = positions.astype(jnp.float32)[:, None] * frequency[None, :]
    return (jnp.cos(angles)[:, None, :], jnp.sin(angles)[:, None, :])


def rotate(values, cosine, sine_part):
    half_size = values.shape[-1] // 2
    leading = values[..., :half_size]
    trailing = values[..., half_size:]
    return jnp.concatenate(
        [leading * cosine - trailing * sine_part, trailing * cosine + leading * sine_part], axis=-1
    )


def gelu_tanh(values):
    return jax.nn.gelu(values, approximate=True)


def local(inputs, w_query, w_key, w_value, w_out, w_up, w_down, gain_attn, gain_ffn, cotangent):
    query_full, key_full, value_full, out_full, up_full, down_full, gain_a_low, gain_f_low = (
        lax.all_gather(w_query, ("dp", "ctx"), axis=0, tiled=True),
        lax.all_gather(w_key, ("dp", "ctx"), axis=0, tiled=True),
        lax.all_gather(w_value, ("dp", "ctx"), axis=0, tiled=True),
        lax.all_gather(w_out, ("dp", "ctx"), axis=1, tiled=True),
        lax.all_gather(w_up, ("dp", "ctx"), axis=0, tiled=True),
        lax.all_gather(w_down, ("dp", "ctx"), axis=2, tiled=True),
        lax.all_gather(gain_attn, ("dp", "ctx"), axis=0, tiled=True),
        lax.all_gather(gain_ffn, ("dp", "ctx"), axis=0, tiled=True),
    )
    gain_first = gain_a_low.astype(jnp.float32)
    gain_second = gain_f_low.astype(jnp.float32)
    inputs_all, cotangent_all = (
        lax.all_gather(inputs, "mp", axis=1, tiled=True),
        lax.all_gather(cotangent, "mp", axis=1, tiled=True),
    )
    count = inputs_all.shape[0]
    length_half = inputs_all.shape[1]
    width = inputs_all.shape[2]
    shard_len = inputs.shape[1]
    total_rows = count * length_half
    mp_count = lax.axis_size("mp")
    mp_index = lax.axis_index("mp")
    ctx_index = lax.axis_index("ctx")
    head_count = query_full.shape[1] // HEAD
    factor = HEAD ** (-0.5)
    positions = ctx_index * length_half + jnp.arange(length_half, dtype=jnp.int32)
    cosine, sine_part = rotation(positions, HEAD)
    inputs_f = inputs_all.astype(jnp.float32)
    flat_first = normalize(inputs_f, gain_first).astype(jnp.bfloat16).reshape(total_rows, width)

    def project(matrix):
        return jnp.dot(flat_first, matrix, preferred_element_type=jnp.float32).reshape(
            count, length_half, head_count, HEAD
        )

    query_rows = rotate(project(query_full), cosine, sine_part).astype(jnp.bfloat16)
    key_rows = rotate(project(key_full), cosine, sine_part).astype(jnp.bfloat16)
    value_rows = project(value_full).astype(jnp.bfloat16)
    early_keys, early_values = from_behind((key_rows, value_rows), "ctx", 1)
    row_ids = jnp.arange(length_half)[:, None]
    col_ids = jnp.arange(2 * length_half)[None, :]
    visible = jnp.where(col_ids < length_half, ctx_index >= 1, col_ids - length_half <= row_ids)

    def scores_of(query_one, keys_all):
        raw_scores = (
            jnp.einsum("qhd,khd->hqk", query_one, keys_all, preferred_element_type=jnp.float32)
            * factor
        )
        return jnp.where(visible[None], raw_scores, NEGATIVE)

    def attend(package):
        query_one, key_one, value_one, key_early, value_early = package
        keys_all = jnp.concatenate([key_early, key_one], 0)
        values_all = jnp.concatenate([value_early, value_one], 0)
        scores = scores_of(query_one, keys_all)
        largest = jnp.max(scores, axis=-1, keepdims=True)
        exponent = jnp.exp(scores - largest)
        totals = jnp.sum(exponent, axis=-1, keepdims=True)
        softened = exponent / totals
        mixed_one = jnp.einsum(
            "hqk,khd->qhd",
            softened.astype(jnp.bfloat16),
            values_all,
            preferred_element_type=jnp.float32,
        )
        return (mixed_one.astype(jnp.bfloat16), (largest + jnp.log(totals))[..., 0])

    mixed_rows, log_totals = lax.map(
        attend, (query_rows, key_rows, value_rows, early_keys, early_values)
    )
    mixed_flat = mixed_rows.reshape(total_rows, head_count * HEAD)
    attended = lax.psum(jnp.dot(mixed_flat, out_full, preferred_element_type=jnp.float32), "mp")
    hidden_state = inputs_f + attended.reshape(count, length_half, width)
    normed_second = (
        normalize(hidden_state, gain_second).astype(jnp.bfloat16).reshape(total_rows, width)
    )
    cot_flat = cotangent_all.reshape(total_rows, width)
    block_width = up_full.shape[2]
    block_total = up_full.shape[1]

    def ffn_both(rows, grad_rows, blocks):
        used = blocks * block_width
        up_part = up_full[:, :blocks].reshape(width, used)
        down_part = down_full[:blocks].reshape(used, width)
        upped = jnp.dot(rows, up_part, preferred_element_type=jnp.float32)
        activated, gelu_pull = jax.vjp(gelu_tanh, upped)
        activated_low = activated.astype(jnp.bfloat16)
        result = jnp.dot(activated_low, down_part, preferred_element_type=jnp.float32)
        grad_act = jnp.einsum("rd,wd->rw", grad_rows, down_part, preferred_element_type=jnp.float32)
        grad_upped = gelu_pull(grad_act)[0].astype(jnp.bfloat16)
        grad_down_part = jnp.einsum(
            "rw,rd->wd", activated_low, grad_rows, preferred_element_type=jnp.float32
        )
        grad_up_part = jnp.einsum("rd,rw->dw", rows, grad_upped, preferred_element_type=jnp.float32)
        grad_in = jnp.einsum("rw,dw->rd", grad_upped, up_part, preferred_element_type=jnp.float32)
        grad_up_pad = jnp.pad(
            grad_up_part.reshape(width, blocks, block_width),
            ((0, 0), (0, block_total - blocks), (0, 0)),
        )
        grad_down_pad = jnp.pad(
            grad_down_part.reshape(blocks, block_width, width),
            ((0, block_total - blocks), (0, 0), (0, 0)),
        )
        return (result, grad_in, grad_up_pad, grad_down_pad)

    def make_branch(blocks):

        def branch_run(rows, grad_rows):
            return ffn_both(rows, grad_rows, blocks)

        return branch_run

    grain = lax.axis_index("dp") % 4
    ffn_part, grad_second_part, grad_up_sum, grad_down_sum = lax.switch(
        grain, [make_branch(2**grain_level) for grain_level in range(4)], normed_second, cot_flat
    )
    grad_second_part = grad_second_part.reshape(count, length_half, width)
    gain_second_part = jnp.sum(grad_second_part * unit_rows(hidden_state), axis=(0, 1))
    ffn_shard, grad_second_shard, gain_second_sum = (
        lax.psum_scatter(
            ffn_part.reshape(count, length_half, width), "mp", scatter_dimension=1, tiled=True
        ),
        lax.psum_scatter(grad_second_part, "mp", scatter_dimension=1, tiled=True),
        lax.psum_scatter(
            jnp.broadcast_to(gain_second_part, (mp_count, width)),
            "mp",
            scatter_dimension=0,
            tiled=True,
        ),
    )
    gain_second_grad = gain_second_sum[0]
    hidden_shard = lax.dynamic_slice_in_dim(hidden_state, mp_index * shard_len, shard_len, 1)
    outputs = (hidden_shard + ffn_shard).astype(jnp.bfloat16)
    grad_hidden_shard = cotangent.astype(jnp.float32) + norm_back(
        hidden_shard, gain_second, grad_second_shard
    )
    grad_hidden_low = lax.all_gather(
        grad_hidden_shard.astype(jnp.bfloat16), "mp", axis=1, tiled=True
    ).reshape(total_rows, width)
    grad_out_w = jnp.einsum(
        "rc,rd->cd", mixed_flat, grad_hidden_low, preferred_element_type=jnp.float32
    )
    grad_mixed = jnp.einsum(
        "rd,cd->rc", grad_hidden_low, out_full, preferred_element_type=jnp.float32
    )
    grad_mixed = grad_mixed.astype(jnp.bfloat16).reshape(count, length_half, head_count, HEAD)

    def attend_back(package):
        query_one, key_one, value_one, key_early, value_early, log_one, grad_one = package
        keys_all = jnp.concatenate([key_early, key_one], 0)
        values_all = jnp.concatenate([value_early, value_one], 0)
        scores = scores_of(query_one, keys_all)
        softened = jnp.exp(scores - log_one[..., None])
        grad_soft = jnp.einsum(
            "qhd,khd->hqk", grad_one, values_all, preferred_element_type=jnp.float32
        )
        grad_values = jnp.einsum(
            "hqk,qhd->khd",
            softened.astype(jnp.bfloat16),
            grad_one,
            preferred_element_type=jnp.float32,
        )
        inner = jnp.sum(grad_soft * softened, axis=-1, keepdims=True)
        grad_scores = (softened * (grad_soft - inner)).astype(jnp.bfloat16)
        grad_queries = (
            jnp.einsum("hqk,khd->qhd", grad_scores, keys_all, preferred_element_type=jnp.float32)
            * factor
        )
        grad_keys = (
            jnp.einsum("hqk,qhd->khd", grad_scores, query_one, preferred_element_type=jnp.float32)
            * factor
        )
        return (
            grad_queries,
            grad_keys[length_half:],
            grad_keys[:length_half],
            grad_values[length_half:],
            grad_values[:length_half],
        )

    grad_queries, grad_key_own, grad_key_early, grad_value_own, grad_value_early = lax.map(
        attend_back,
        (query_rows, key_rows, value_rows, early_keys, early_values, log_totals, grad_mixed),
    )
    key_back, value_back = (
        from_behind(grad_key_early.astype(jnp.bfloat16), "ctx", -1).astype(grad_key_early.dtype),
        from_behind(grad_value_early.astype(jnp.bfloat16), "ctx", -1).astype(
            grad_value_early.dtype
        ),
    )
    grad_query_low = (
        rotate(grad_queries, cosine, -sine_part).astype(jnp.bfloat16).reshape(total_rows, -1)
    )
    grad_key_low = (
        rotate(grad_key_own + key_back, cosine, -sine_part)
        .astype(jnp.bfloat16)
        .reshape(total_rows, -1)
    )
    grad_value_low = (grad_value_own + value_back).astype(jnp.bfloat16).reshape(total_rows, -1)
    grad_query_w = jnp.einsum(
        "rd,rc->dc", flat_first, grad_query_low, preferred_element_type=jnp.float32
    )
    grad_key_w = jnp.einsum(
        "rd,rc->dc", flat_first, grad_key_low, preferred_element_type=jnp.float32
    )
    grad_value_w = jnp.einsum(
        "rd,rc->dc", flat_first, grad_value_low, preferred_element_type=jnp.float32
    )
    grad_first_part = jnp.einsum(
        "rc,dc->rd", grad_query_low, query_full, preferred_element_type=jnp.float32
    )
    grad_first_part = grad_first_part + jnp.einsum(
        "rc,dc->rd", grad_key_low, key_full, preferred_element_type=jnp.float32
    )
    grad_first_part = grad_first_part + jnp.einsum(
        "rc,dc->rd", grad_value_low, value_full, preferred_element_type=jnp.float32
    )
    grad_first_part = grad_first_part.reshape(count, length_half, width)
    gain_first_part = jnp.sum(grad_first_part * unit_rows(inputs_f), axis=(0, 1))
    grad_first_shard, gain_first_sum = (
        lax.psum_scatter(
            grad_first_part.astype(jnp.bfloat16), "mp", scatter_dimension=1, tiled=True
        ).astype(jnp.float32),
        lax.psum_scatter(
            jnp.broadcast_to(gain_first_part, (mp_count, width)).astype(jnp.bfloat16),
            "mp",
            scatter_dimension=0,
            tiled=True,
        ).astype(jnp.float32),
    )
    input_grads = grad_hidden_shard + norm_back(
        inputs.astype(jnp.float32), gain_first, grad_first_shard
    )
    (
        grad_query_out,
        grad_key_out,
        grad_value_out,
        grad_out_out,
        grad_up_out,
        grad_down_out,
        gain_attn_out,
        gain_ffn_out,
    ) = (
        lax.psum_scatter(grad_query_w, ("dp", "ctx"), scatter_dimension=0, tiled=True),
        lax.psum_scatter(grad_key_w, ("dp", "ctx"), scatter_dimension=0, tiled=True),
        lax.psum_scatter(grad_value_w, ("dp", "ctx"), scatter_dimension=0, tiled=True),
        lax.psum_scatter(grad_out_w, ("dp", "ctx"), scatter_dimension=1, tiled=True),
        lax.psum_scatter(grad_up_sum, ("dp", "ctx"), scatter_dimension=0, tiled=True),
        lax.psum_scatter(grad_down_sum, ("dp", "ctx"), scatter_dimension=2, tiled=True),
        lax.psum_scatter(gain_first_sum[0], ("dp", "ctx"), scatter_dimension=0, tiled=True),
        lax.psum_scatter(gain_second_grad, ("dp", "ctx"), scatter_dimension=0, tiled=True),
    )
    return (
        outputs,
        input_grads,
        grad_query_out,
        grad_key_out,
        grad_value_out,
        grad_out_out,
        grad_up_out,
        grad_down_out,
        gain_attn_out,
        gain_ffn_out,
    )


def solution(mesh):
    in_specs = (
        P("dp", ("ctx", "mp"), None),
        P(("dp", "ctx"), "mp"),
        P(("dp", "ctx"), "mp"),
        P(("dp", "ctx"), "mp"),
        P("mp", ("dp", "ctx")),
        P(("dp", "ctx"), None, "mp"),
        P(None, "mp", ("dp", "ctx")),
        P(("dp", "ctx")),
        P(("dp", "ctx")),
        P("dp", ("ctx", "mp"), None),
    )
    out_specs = (
        P("dp", ("ctx", "mp"), None),
        P("dp", ("ctx", "mp"), None),
        P(("dp", "ctx"), "mp"),
        P(("dp", "ctx"), "mp"),
        P(("dp", "ctx"), "mp"),
        P("mp", ("dp", "ctx")),
        P(("dp", "ctx"), None, "mp"),
        P(None, "mp", ("dp", "ctx")),
        P(("dp", "ctx")),
        P(("dp", "ctx")),
    )
    return jax.shard_map(local, mesh=mesh, in_specs=in_specs, out_specs=out_specs, check_vma=False)
```

profile of v0, /device:TPU:0, one launch (start us, length us, event | category | flops | bytes accessed | tf_op | source)
XLA Modules:
  0.0 1783.2 jit_solution(12301022891588044339)
XLA Ops:
  13.7 15.5 all-reduce.13
  30.5 6.4 all-gather.16.cloned.1.call-done
  38.4 24.4 %all-gather.14.cloned.1.call-done = bf16[1536,384]{1,0:T(8,128)(2,1)} async-done(((bf16[192,384]{1,0:T(8,128)(2,1)}), bf16[1536,384]{1,0:T(8,128)(2,1)}) %all-gather.14.cloned.1.call-update) | async-done | bytes 1179664 | tf_op jit(solution)/shard_map/all_gather | solution.py:56
  64.4 24.4 %all-gather.12.cloned.1.call-done = bf16[1536,384]{1,0:T(8,128)(2,1)} async-done(((bf16[192,384]{1,0:T(8,128)(2,1)}), bf16[1536,384]{1,0:T(8,128)(2,1)}) %all-gather.12.cloned.1.call-update) | async-done | bytes 1179664 | tf_op jit(solution)/shard_map/all_gather | solution.py:58
  91.2 88.5 %all-gather.10.cloned.1.call-done = bf16[3,512,1536]{2,1,0:T(8,128)(2,1)} async-done(((bf16[3,128,1536]{2,1,0:T(8,128)(2,1)}), bf16[3,512,1536]{2,1,0:T(8,128)(2,1)}) %all-gather.10.cloned.1.call-update) | async-done | bytes 4718608 | tf_op jit(solution)/shard_map/all_gather | solution.py:68
  207.8 42.8 %while.32 = (s32[]{:T(128)}, bf16[3,512,3,128]{1,3,2,0:T(8,128)(2,1)}, f32[3,3,512]{2,1,0:T(4,128)}, bf16[3,512,3,128]{3,1,2,0:T(8,128)(2,1)}, bf16[3,512,3,128]...) while((s32[]{:T(128)}, ...), condition=%wide.region_4.5_spmd.clone, body=%wide.region_1.4_spmd.clone.sunk | while | flops 828570112 | bytes 53273240 | solution.py:123
  216.4 5.6 fusion.228
  230.7 5.6 fusion.228
  244.9 5.6 fusion.228
  254.4 8.0 fusion.133
  266.0 319.7 %all-reduce.16.cloned.1.call-done = f32[3,512,1536]{2,1,0:T(8,128)} async-done(((f32[3,512,1536]{2,1,0:T(8,128)}), f32[3,512,1536]{2,1,0:T(8,128)}) %all-reduce.16.cloned.1.call-update) | async-done | bytes 9437200 | tf_op jit(solution)/shard_map/psum | solution.py:127
  585.7 10.6 multiply_reduce_fusion.2
  596.9 6.7 multiply_convert_fusion.13
  603.6 72.0 %all-gather.24.cloned.1.call-done = bf16[3,512,1536]{2,1,0:T(8,128)(2,1)} async-done(((bf16[3,128,1536]{2,1,0:T(8,128)(2,1)}), bf16[3,512,1536]{2,1,0:T(8,128)(2,1)}) %all-gather.24.cloned.1.call-update) | async-done | bytes 4718608 | tf_op jit(solution)/shard_map/all_gather | solution.py:69
  675.7 46.5 %all-gather.22.cloned.1.call-done = bf16[8,192,1536]{1,0,2:T(8,128)(2,1)} async-done(((bf16[8,192,192]{1,0,2:T(8,128)(2,1)}), bf16[8,192,1536]{1,0,2:T(8,128)(2,1)}) %all-gather.22.cloned.1.call-update) | async-done | bytes 4718608 | tf_op jit(solution)/shard_map/all_gather | solution.py:61
  722.1 47.4 %all-gather.20.cloned.1.call-done = bf16[1536,8,192]{2,1,0:T(8,128)(2,1)} async-done(((bf16[192,8,192]{2,1,0:T(8,128)(2,1)}), bf16[1536,8,192]{2,1,0:T(8,128)(2,1)}) %all-gather.20.cloned.1.call-update) | async-done | bytes 4718608 | tf_op jit(solution)/shard_map/all_gather | solution.py:60
  769.6 72.1 %conditional.1 = (f32[1536,1536]{1,0:T(8,128)}, f32[1536,1536]{1,0:T(8,128)}, f32[1536,8,192]{0,2,1:T(8,128)}, f32[8,192,1536]{2,1,0:T(8,128)}) conditional(s32[]{:T(128)} %clamp.3, (bf16[1536,8,192]{2,1,0:T(8,128)(2,1)}, bf16[1536,1536]{1,0:T(8,128)(2,1)}, bf16[8,192,1536]{1,0,2:T(8,128)(2,1)}, ...), branch_computations={%region_7.8_spmd, %region_8.9_spmd, %region_9.10_spmd, %region_10.... | conditional | flops 43576197120 | bytes 273678624 | solution.py:169
  769.7 8.8 copy.70
  782.7 8.8 copy.71
  791.5 4.7 fusion.10
  796.2 6.1 fusion.11
  803.4 4.7 pad.18
  808.1 6.3 fusion.14
  815.6 4.8 pad.19
  841.8 204.0 %reduce-scatter.14.cloned.1.call-done = f32[3,128,1536]{2,1,0:T(8,128)} async-done(((f32[3,512,1536]{2,1,0:T(8,128)}), f32[3,128,1536]{2,1,0:T(8,128)}) %reduce-scatter.14.cloned.1.call-update) | async-done | bytes 2359312 | tf_op jit(solution)/shard_map/reduce_scatter | solution.py:178
  1052.9 12.9 copy.90
  1065.8 13.1 reshape.343
  1079.0 64.2 %all-gather.26.cloned.1.call-done = bf16[3,512,1536]{2,1,0:T(8,128)(2,1)} async-done(((bf16[3,128,1536]{2,1,0:T(8,128)(2,1)}), bf16[3,512,1536]{2,1,0:T(8,128)(2,1)}) %all-gather.26.cloned.1.call-update) | async-done | bytes 4718608 | tf_op jit(solution)/shard_map/all_gather | solution.py:192
  1143.2 4.9 convolution_convert_fusion
  1151.9 52.4 %while.33 = (s32[]{:T(128)}, f32[3,512,3,128]{1,3,2,0:T(8,128)}, f32[3,512,3,128]{1,3,2,0:T(8,128)}, bf16[3,512,3,128]{1,3,2,0:T(8,128)(2,1)}, f32[3,512,3,128]{...) while((s32[]{:T(128)}, f32[3,512,3,128]{1,3,2,0:T(8,128)}, ...), condition=%wide.region_18.19_spmd.clone, body=%wide.region_16.18_spmd.clone.sunk | while | flops 2043214336 | bytes 65065664 | solution.py:236
  1227.9 4.5 fusion.129
  1244.9 12.9 copy.85
  1258.3 6.9 fusion.131
  1265.3 6.4 fusion.121
  1271.8 6.4 fusion.124
  1279.6 6.5 fusion.127
  1288.0 7.4 multiply_reduce_fusion.1
  1295.4 19.1 %all-reduce.10 = f32[4,1536]{1,0:T(4,128)S(1)} all-reduce(f32[4,1536]{1,0:T(4,128)S(1)} %broadcast_in_dim.98), channel_id=13, replica_groups=mesh['dp'=4,'ctx'=2,'mp'=4] {'mp'}, use_global_device_ids=true, to_apply=%region_31.32.clone | all-reduce | flops 6144 | bytes 49152
  1319.4 6.5 fusion.105
  1326.6 17.4 all-reduce.8
  1345.9 23.9 %all-reduce.12 = (f32[1536]{0:T(1024)}, f32[1536]{0:T(1024)}) all-reduce(f32[1536]{0:T(1024)} %fusion.144, f32[1536]{0:T(1024)} %dynamic-slice_reduce_fusion), channel_id=12, replica_groups=mesh['dp'=4,'ctx'=2,'mp'=4] {'dp','ctx'}, use_global_device_ids=true, to_apply=%region_29.30.clone | all-reduce | flops 3072 | bytes 24576
  1375.5 117.7 %reduce-scatter.12.cloned.1.call-done = f32[3,128,1536]{2,1,0:T(8,128)} async-done(((f32[3,512,1536]{2,1,0:T(8,128)}), f32[3,128,1536]{2,1,0:T(8,128)}) %reduce-scatter.12.cloned.1.call-update) | async-done | bytes 2359312 | tf_op jit(solution)/shard_map/reduce_scatter | solution.py:175
  1493.2 5.1 fusion.116
  1498.3 92.1 %reduce-scatter.26.cloned.1.call-done = f32[192,8,192]{2,1,0:T(8,128)} async-done(((f32[1536,8,192]{2,1,0:T(8,128)}), f32[192,8,192]{2,1,0:T(8,128)}) %reduce-scatter.26.cloned.1.call-update) | async-done | bytes 1179664 | tf_op jit(solution)/shard_map/reduce_scatter | solution.py:303
  1590.4 46.3 %reduce-scatter.24.cloned.1.call-done = f32[384,192]{0,1:T(8,128)} async-done(((f32[384,1536]{0,1:T(8,128)}), f32[384,192]{0,1:T(8,128)}) %reduce-scatter.24.cloned.1.call-update) | async-done | bytes 294928 | tf_op jit(solution)/shard_map/reduce_scatter | solution.py:302
  1636.7 46.6 %reduce-scatter.22.cloned.1.call-done = f32[192,384]{1,0:T(8,128)} async-done(((f32[1536,384]{1,0:T(8,128)}), f32[192,384]{1,0:T(8,128)}) %reduce-scatter.22.cloned.1.call-update) | async-done | bytes 294928 | tf_op jit(solution)/shard_map/reduce_scatter | solution.py:301
  1683.4 46.3 %reduce-scatter.20.cloned.1.call-done = f32[192,384]{1,0:T(8,128)} async-done(((f32[1536,384]{1,0:T(8,128)}), f32[192,384]{1,0:T(8,128)}) %reduce-scatter.20.cloned.1.call-update) | async-done | bytes 294928 | tf_op jit(solution)/shard_map/reduce_scatter | solution.py:300
  1729.7 46.8 %reduce-scatter.18.cloned.1.call-done = f32[192,384]{1,0:T(8,128)} async-done(((f32[1536,384]{1,0:T(8,128)}), f32[192,384]{1,0:T(8,128)}) %reduce-scatter.18.cloned.1.call-update) | async-done | bytes 294928 | tf_op jit(solution)/shard_map/reduce_scatter | solution.py:299
  (269 shorter events, 196.0 us)
Async XLA Ops:
  7.2 29.7 %all-gather.16.cloned.1.call-start = ((), (), s32[]{:S(2)}) async-start(), calls=%async_computation.12 | async-start | bytes 1327104 | tf_op jit(solution)/shard_map/all_gather | solution.py:57
  7.9 54.9 %all-gather.14.cloned.1.call-start = ((), (), s32[]{:S(2)}) async-start(), calls=%async_computation.11 | async-start | bytes 1327104 | tf_op jit(solution)/shard_map/all_gather | solution.py:56
  8.7 80.2 %all-gather.12.cloned.1.call-start = ((), (), s32[]{:S(2)}) async-start(), calls=%async_computation.10 | async-start | bytes 1327104 | tf_op jit(solution)/shard_map/all_gather | solution.py:58
  9.4 170.3 %all-gather.10.cloned.1.call-start = ((), (), s32[]{:S(2)}) async-start(), calls=%async_computation.9 | async-start | bytes 5898240 | tf_op jit(solution)/shard_map/all_gather | solution.py:68
  10.0 244.5 %all-gather.18.cloned.1.call-start = ((), (), s32[]{:S(2)}) async-start(), calls=%async_computation.13 | async-start | bytes 1327104 | tf_op jit(solution)/shard_map/all_gather | solution.py:59
  29.3 153.9 %copy-start.25 = (f32[1536]{0:T(1024)}, f32[1536]{0:T(1024)S(1)}, u32[]{:S(2)}) copy-start(f32[1536]{0:T(1024)S(1)} %convert_element_type.148) | copy-start | bytes 18436
  30.5 158.2 %copy-start.14 = (f32[512,64]{0,1:T(8,128)}, f32[512,64]{0,1:T(8,128)S(1)}, u32[]{:S(2)}) copy-start(f32[512,64]{0,1:T(8,128)S(1)} %get-tuple-element.456) | copy-start | bytes 393220
  179.7 3.8 copy-start.2
  184.6 8.7 copy-start.12
  190.4 14.9 collective-permute-start.1
  197.0 10.7 collective-permute-start
  199.4 386.2 %all-reduce.16.cloned.1.call-start = ((), (), s32[]{:S(2)}) async-start(), calls=%async_computation.14 | async-start | bytes 18874368 | tf_op jit(solution)/shard_map/psum | solution.py:127
  250.6 11.9 copy-start.3
  250.6 11.9 copy-start.20
  250.6 11.9 copy-start.27
  262.5 413.2 %all-gather.24.cloned.1.call-start = ((), (), s32[]{:S(2)}) async-start(), calls=%async_computation.17 | async-start | bytes 5898240 | tf_op jit(solution)/shard_map/all_gather | solution.py:69
  263.2 458.9 %all-gather.22.cloned.1.call-start = ((), (), s32[]{:S(2)}) async-start(), calls=%async_computation.16 | async-start | bytes 7077888 | tf_op jit(solution)/shard_map/all_gather | solution.py:61
  265.1 504.4 %all-gather.20.cloned.1.call-start = ((), (), s32[]{:S(2)}) async-start(), calls=%async_computation.15 | async-start | bytes 7077888 | tf_op jit(solution)/shard_map/all_gather | solution.py:60
  265.9 779.9 %reduce-scatter.14.cloned.1.call-start = ((), (), s32[]{:S(2)}) async-start(), calls=%async_computation.19 | async-start | bytes 11796480 | tf_op jit(solution)/shard_map/reduce_scatter | solution.py:178
  265.9 330.4 %copy-start.22 = (f32[1536]{0:T(1024)}, f32[1536]{0:T(1024)S(1)}, u32[]{:S(2)}) copy-start(f32[1536]{0:T(1024)S(1)} %convert_element_type.152) | copy-start | bytes 18436
  782.7 19.6 %slice-start = ((s8[4718592]{0:T(1024)(128)(4,1)}), s8[524288]{0:T(1024)(128)(4,1)S(1)}, s32[]{:S(2)}) async-start(s8[4718592]{0:T(1024)(128)(4,1)} %bitcast.266), calls=%async_computation.28 | async-start | bytes 1048576 | tf_op jit(solution)/shard_map/cond
  791.5 10.8 slice-start.1
  803.4 11.0 slice-start.10
  808.1 6.3 slice-start.11
  841.7 204.1 %copy-start.23 = (f32[1536]{0:T(1024)S(1)}, f32[1536]{0:T(1024)}, u32[]{:S(2)}) copy-start(f32[1536]{0:T(1024)} %copy-done.22) | copy-start | bytes 18436
  841.7 301.5 %all-gather.26.cloned.1.call-start = ((), (), s32[]{:S(2)}) async-start(), calls=%async_computation.20 | async-start | bytes 5898240 | tf_op jit(solution)/shard_map/all_gather | solution.py:192
  841.7 207.7 %copy-start.8 = (bf16[3,128,1536]{2,1,0:T(8,128)(2,1)S(1)}, bf16[3,128,1536]{2,1,0:T(8,128)(2,1)}, u32[]{:S(2)}) copy-start(bf16[3,128,1536]{2,1,0:T(8,128)(2,1)} %param.27) | copy-start | bytes 3538948
  1045.8 3.6 copy-start.5
  1052.8 262.9 %reduce-scatter.28.cloned.1.call-start = ((), (), s32[]{:S(2)}) async-start(), calls=%async_computation.27 | async-start | bytes 10616832
  1078.9 64.3 %copy-start.16 = (bf16[384,1536]{0,1:T(8,128)(2,1)S(1)}, bf16[384,1536]{0,1:T(8,128)(2,1)}, u32[]{:S(2)}) copy-start(bf16[384,1536]{0,1:T(8,128)(2,1)} %all-gather.18.cloned.1.call-done) | copy-start | bytes 3538948
  1079.0 293.5 %reduce-scatter.16.cloned.1.call-start = ((), (), s32[]{:S(2)}) async-start(), calls=%async_computation.21 | async-start | bytes 5898240 | tf_op jit(solution)/shard_map/reduce_scatter | solution.py:276
  1148.2 3.7 copy-start.4
  1148.2 3.7 copy-start.21
  1148.2 3.7 copy-start.28
  1204.3 4.7 collective-permute-start.3
  1205.6 6.6 collective-permute-start.2
  1227.9 4.5 copy-start.10
  1244.2 249.0 %reduce-scatter.12.cloned.1.call-start = ((), (), s32[]{:S(2)}) async-start(), calls=%async_computation.18 | async-start | bytes 11796480 | tf_op jit(solution)/shard_map/reduce_scatter | solution.py:175
  1244.8 345.6 %reduce-scatter.26.cloned.1.call-start = ((), (), s32[]{:S(2)}) async-start(), calls=%async_computation.26 | async-start | bytes 14155776 | tf_op jit(solution)/shard_map/reduce_scatter | solution.py:303
  1257.8 378.9 %reduce-scatter.24.cloned.1.call-start = ((), (), s32[]{:S(2)}) async-start(), calls=%async_computation.25 | async-start | bytes 2654208 | tf_op jit(solution)/shard_map/reduce_scatter | solution.py:302
  1265.2 418.1 %reduce-scatter.22.cloned.1.call-start = ((), (), s32[]{:S(2)}) async-start(), calls=%async_computation.24 | async-start | bytes 2654208 | tf_op jit(solution)/shard_map/reduce_scatter | solution.py:301
  1271.7 457.9 %reduce-scatter.20.cloned.1.call-start = ((), (), s32[]{:S(2)}) async-start(), calls=%async_computation.23 | async-start | bytes 2654208 | tf_op jit(solution)/shard_map/reduce_scatter | solution.py:300
  1278.2 498.2 %reduce-scatter.18.cloned.1.call-start = ((), (), s32[]{:S(2)}) async-start(), calls=%async_computation.22 | async-start | bytes 2654208 | tf_op jit(solution)/shard_map/reduce_scatter | solution.py:299
  1315.7 3.7 copy-start.30
  1319.4 53.1 %copy-start.7 = (bf16[3,128,1536]{2,1,0:T(8,128)(2,1)S(1)}, bf16[3,128,1536]{2,1,0:T(8,128)(2,1)}, u32[]{:S(2)}) copy-start(bf16[3,128,1536]{2,1,0:T(8,128)(2,1)} %param.18) | copy-start | bytes 3538948
  1319.4 53.1 %copy-start.26 = (f32[1536]{0:T(1024)S(1)}, f32[1536]{0:T(1024)}, u32[]{:S(2)}) copy-start(f32[1536]{0:T(1024)} %copy-done.25) | copy-start | bytes 18436
  1326.0 167.3 %copy-start.6 = (f32[3,128,1536]{2,1,0:T(8,128)S(1)}, f32[3,128,1536]{2,1,0:T(8,128)}, u32[]{:S(2)}) copy-start(f32[3,128,1536]{2,1,0:T(8,128)} %reduce-scatter.14.cloned.1.call-done) | copy-start | bytes 7077892
  1326.0 167.2 %copy-start.24 = (f32[1536]{0:T(1024)S(1)}, f32[1536]{0:T(1024)}, u32[]{:S(2)}) copy-start(f32[1536]{0:T(1024)} %copy-done.22) | copy-start | bytes 18436
  (17 other events, 30.9 us)
Sparse Core Ops, SparseCore 0:
  9.9 26.9 all-gather.15
  38.8 24.0 all-gather.13
  64.7 24.0 all-gather.11
  90.3 89.3 all-gather.9
  199.5 22.5 all-gather.17
  262.6 323.0 all-reduce.15
  587.2 88.3 all-gather.23
  678.1 43.9 all-gather.21
  724.0 45.5 all-gather.19
  841.8 203.9 reduce-scatter.13
  1052.9 90.2 all-gather.25
  1146.6 74.9 reduce-scatter.27
  1244.4 84.7 reduce-scatter.15
  1331.3 161.8 reduce-scatter.11
  1497.1 93.2 reduce-scatter.25
  1594.2 42.4 reduce-scatter.23
  1640.9 42.4 reduce-scatter.21
  1687.1 42.4 reduce-scatter.19
  1734.0 42.4 reduce-scatter.17
where the time goes:
time: 1790 us; the launch traced here: 1780 us
  waiting for transfers between devices  1300 us (73%)
  local copies, waits for them, and re-layouts  144 us (8%)
  matrix products  128 us (7%)
  other arithmetic  87.2 us (5%)
  blocking collectives  75.9 us (4%)
  loops' own time  21.7 us (1%)
    psum x1, waiting for transfers between devices, local(): lax.psum(jnp.dot(mixed_flat, out_full, preferred_element_type=jnp.float32...  320 us
    reduce_scatter x1, waiting for transfers between devices, local(): lax.psum_scatter(grad_second_part, 'mp', scatter_dimension=1, tiled=True)  204 us
    reduce_scatter x1, waiting for transfers between devices, local(): lax.psum_scatter(ffn_part.reshape(count, length_half, width), 'mp', scatt...  118 us
    reduce_scatter x1, waiting for transfers between devices, local(): lax.psum_scatter(grad_up_sum, ('dp', 'ctx'), scatter_dimension=0, tiled=T...  92.1 us
    all_gather x1, waiting for transfers between devices, local(): lax.all_gather(inputs, 'mp', axis=1, tiled=True)  88.5 us
    unnamed x4, blocking collectives  75.9 us
    all_gather x1, waiting for transfers between devices, local(): lax.all_gather(cotangent, 'mp', axis=1, tiled=True)  72 us
    all_gather x1, waiting for transfers between devices, local(): lax.all_gather(grad_hidden_shard.astype(jnp.bfloat16), 'mp', axis=1, tile...  64.2 us
  transfers between devices with their start and end apart: 23, of which 17 were waited for; matrix products, arithmetic and copies ran while one was open for 15% of the time, Pallas kernels for 0%

commit v1 on v0

--- a/solution.py
+++ b/solution.py
@@ -124,7 +124,10 @@
         attend, (query_rows, key_rows, value_rows, early_keys, early_values)
     )
     mixed_flat = mixed_rows.reshape(total_rows, head_count * HEAD)
-    attended = lax.psum(jnp.dot(mixed_flat, out_full, preferred_element_type=jnp.float32), "mp")
+    attended = jnp.sum(
+        lax.all_gather(jnp.dot(mixed_flat, out_full, preferred_element_type=jnp.float32), "mp"),
+        axis=0,
+    )
     hidden_state = inputs_f + attended.reshape(count, length_half, width)
     normed_second = (
         normalize(hidden_state, gain_second).astype(jnp.bfloat16).reshape(total_rows, width)

time: 1790 us -> 2100 us (1.17)
  waiting for transfers between devices: 1300 us -> 1590 us
    all_gather x0 -> x1, waiting for transfers between devices: none -> 626 us  [local(): lax.all_gather(jnp.dot(mixed_flat, out_full, preferred_element_type=jnp.f...]
    psum x1 -> x0, waiting for transfers between devices: 320 us -> none  [local(): lax.psum(jnp.dot(mixed_flat, out_full, preferred_element_type=jnp.float32...]
  transfers between devices with their start and end apart: 23 -> 23, of which waited for: 17 -> 17; matrix products, arithmetic and copies ran while one was open for 15% -> 14% of each run, Pallas kernels for 0% -> 0%
where the time goes in v1:
time: 2100 us; the launch traced here: 2090 us
  waiting for transfers between devices  1590 us (76%)
  local copies, waits for them, and re-layouts  144 us (7%)
  matrix products  128 us (6%)
  other arithmetic  106 us (5%)
  blocking collectives  75.8 us (4%)
  loops' own time  21.7 us (1%)
    all_gather x1, waiting for transfers between devices, local(): lax.all_gather(jnp.dot(mixed_flat, out_full, preferred_element_type=jnp.f...  626 us
    reduce_scatter x1, waiting for transfers between devices, local(): lax.psum_scatter(grad_second_part, 'mp', scatter_dimension=1, tiled=True)  204 us
    reduce_scatter x1, waiting for transfers between devices, local(): lax.psum_scatter(ffn_part.reshape(count, length_half, width), 'mp', scatt...  118 us
    reduce_scatter x1, waiting for transfers between devices, local(): lax.psum_scatter(grad_up_sum, ('dp', 'ctx'), scatter_dimension=0, tiled=T...  92 us
    all_gather x1, waiting for transfers between devices, local(): lax.all_gather(inputs, 'mp', axis=1, tiled=True)  88.5 us
    unnamed x4, blocking collectives  75.8 us
    all_gather x1, waiting for transfers between devices, local(): lax.all_gather(grad_hidden_shard.astype(jnp.bfloat16), 'mp', axis=1, tile...  64.2 us
    all_gather x1, waiting for transfers between devices, local(): lax.all_gather(cotangent, 'mp', axis=1, tiled=True)  52.7 us
  transfers between devices with their start and end apart: 23, of which 17 were waited for; matrix products, arithmetic and copies ran while one was open for 14% of the time, Pallas kernels for 0%

profile of v1, /device:TPU:0, one launch (start us, length us, event | category | flops | bytes accessed | tf_op | source)
XLA Modules:
  0.0 2089.8 jit_solution(15448360332707482137)
XLA Ops:
  13.8 15.5 all-reduce.13
  30.5 6.3 all-gather.18.cloned.1.call-done
  38.4 24.4 %all-gather.16.cloned.1.call-done = bf16[1536,384]{1,0:T(8,128)(2,1)} async-done(((bf16[192,384]{1,0:T(8,128)(2,1)}), bf16[1536,384]{1,0:T(8,128)(2,1)}) %all-gather.16.cloned.1.call-update) | async-done | bytes 1179664 | tf_op jit(solution)/shard_map/all_gather | solution.py:56
  64.4 24.4 %all-gather.14.cloned.1.call-done = bf16[1536,384]{1,0:T(8,128)(2,1)} async-done(((bf16[192,384]{1,0:T(8,128)(2,1)}), bf16[1536,384]{1,0:T(8,128)(2,1)}) %all-gather.14.cloned.1.call-update) | async-done | bytes 1179664 | tf_op jit(solution)/shard_map/all_gather | solution.py:58
  91.2 88.5 %all-gather.12.cloned.1.call-done = bf16[3,512,1536]{2,1,0:T(8,128)(2,1)} async-done(((bf16[3,128,1536]{2,1,0:T(8,128)(2,1)}), bf16[3,512,1536]{2,1,0:T(8,128)(2,1)}) %all-gather.12.cloned.1.call-update) | async-done | bytes 4718608 | tf_op jit(solution)/shard_map/all_gather | solution.py:68
  207.5 42.9 %while.32 = (s32[]{:T(128)}, bf16[3,512,3,128]{1,3,2,0:T(8,128)(2,1)}, f32[3,3,512]{2,1,0:T(4,128)}, bf16[3,512,3,128]{3,1,2,0:T(8,128)(2,1)}, bf16[3,512,3,128]...) while((s32[]{:T(128)}, ...), condition=%wide.region_4.5_spmd.clone, body=%wide.region_1.4_spmd.clone.sunk | while | flops 828570112 | bytes 53273240 | solution.py:123
  216.2 5.6 fusion.228
  230.5 5.6 fusion.228
  244.7 5.6 fusion.228
  254.2 8.1 fusion.133
  266.4 626.4 %all-gather.30.cloned.1.call-done = f32[6144,1536]{1,0:T(8,128)} async-done(((f32[1536,1536]{1,0:T(8,128)}), f32[6144,1536]{1,0:T(8,128)}) %all-gather.30.cloned.1.call-update) | async-done | bytes 37748752 | tf_op jit(solution)/shard_map/all_gather | solution.py:128
  892.8 19.6 reduce_sum.108
  912.4 9.9 multiply_reduce_fusion.2
  922.9 6.7 multiply_convert_fusion.13
  929.6 52.7 %all-gather.26.cloned.1.call-done = bf16[3,512,1536]{2,1,0:T(8,128)(2,1)} async-done(((bf16[3,128,1536]{2,1,0:T(8,128)(2,1)}), bf16[3,512,1536]{2,1,0:T(8,128)(2,1)}) %all-gather.26.cloned.1.call-update) | async-done | bytes 4718608 | tf_op jit(solution)/shard_map/all_gather | solution.py:69
  982.4 46.5 %all-gather.24.cloned.1.call-done = bf16[8,192,1536]{1,0,2:T(8,128)(2,1)} async-done(((bf16[8,192,192]{1,0,2:T(8,128)(2,1)}), bf16[8,192,1536]{1,0,2:T(8,128)(2,1)}) %all-gather.24.cloned.1.call-update) | async-done | bytes 4718608 | tf_op jit(solution)/shard_map/all_gather | solution.py:61
  1028.8 47.4 %all-gather.22.cloned.1.call-done = bf16[1536,8,192]{2,1,0:T(8,128)(2,1)} async-done(((bf16[192,8,192]{2,1,0:T(8,128)(2,1)}), bf16[1536,8,192]{2,1,0:T(8,128)(2,1)}) %all-gather.22.cloned.1.call-update) | async-done | bytes 4718608 | tf_op jit(solution)/shard_map/all_gather | solution.py:60
  1076.3 72.0 %conditional.1 = (f32[1536,1536]{1,0:T(8,128)}, f32[1536,1536]{1,0:T(8,128)}, f32[1536,8,192]{0,2,1:T(8,128)}, f32[8,192,1536]{2,1,0:T(8,128)}) conditional(s32[]{:T(128)} %clamp.3, (bf16[1536,8,192]{2,1,0:T(8,128)(2,1)}, bf16[1536,1536]{1,0:T(8,128)(2,1)}, bf16[8,192,1536]{1,0,2:T(8,128)(2,1)}, ...), branch_computations={%region_7.8_spmd, %region_8.9_spmd, %region_9.10_spmd, %region_10.... | conditional | flops 43576197120 | bytes 273678624 | solution.py:172
  1076.4 8.8 copy.70
  1089.4 8.8 copy.71
  1098.2 4.7 fusion.10
  1102.8 6.1 fusion.11
  1110.1 4.7 pad.18
  1114.8 6.3 fusion.14
  1122.3 4.8 pad.19
  1148.4 204.1 %reduce-scatter.14.cloned.1.call-done = f32[3,128,1536]{2,1,0:T(8,128)} async-done(((f32[3,512,1536]{2,1,0:T(8,128)}), f32[3,128,1536]{2,1,0:T(8,128)}) %reduce-scatter.14.cloned.1.call-update) | async-done | bytes 2359312 | tf_op jit(solution)/shard_map/reduce_scatter | solution.py:181
  1359.7 12.9 copy.90
  1372.6 13.1 reshape.344
  1385.8 64.2 %all-gather.28.cloned.1.call-done = bf16[3,512,1536]{2,1,0:T(8,128)(2,1)} async-done(((bf16[3,128,1536]{2,1,0:T(8,128)(2,1)}), bf16[3,512,1536]{2,1,0:T(8,128)(2,1)}) %all-gather.28.cloned.1.call-update) | async-done | bytes 4718608 | tf_op jit(solution)/shard_map/all_gather | solution.py:195
  1450.0 4.9 convolution_convert_fusion
  1458.6 52.4 %while.33 = (s32[]{:T(128)}, f32[3,512,3,128]{1,3,2,0:T(8,128)}, f32[3,512,3,128]{1,3,2,0:T(8,128)}, bf16[3,512,3,128]{1,3,2,0:T(8,128)(2,1)}, f32[3,512,3,128]{...) while((s32[]{:T(128)}, f32[3,512,3,128]{1,3,2,0:T(8,128)}, ...), condition=%wide.region_18.19_spmd.clone, body=%wide.region_16.18_spmd.clone.sunk | while | flops 2043214336 | bytes 65065664 | solution.py:239
  1551.5 12.9 copy.85
  1564.9 6.9 fusion.131
  1572.0 6.4 fusion.121
  1578.5 6.4 fusion.124
  1586.3 6.5 fusion.127
  1594.7 7.4 multiply_reduce_fusion.1
  1602.1 19.0 all-reduce.10
  1626.1 6.5 fusion.105
  1633.2 17.3 all-reduce.8
  1652.6 23.9 %all-reduce.12 = (f32[1536]{0:T(1024)}, f32[1536]{0:T(1024)}) all-reduce(f32[1536]{0:T(1024)} %fusion.144, f32[1536]{0:T(1024)} %dynamic-slice_reduce_fusion), channel_id=13, replica_groups=mesh['dp'=4,'ctx'=2,'mp'=4] {'dp','ctx'}, use_global_device_ids=true, to_apply=%region_29.30.clone | all-reduce | flops 3072 | bytes 24576
  1682.3 117.6 %reduce-scatter.12.cloned.1.call-done = f32[3,128,1536]{2,1,0:T(8,128)} async-done(((f32[3,512,1536]{2,1,0:T(8,128)}), f32[3,128,1536]{2,1,0:T(8,128)}) %reduce-scatter.12.cloned.1.call-update) | async-done | bytes 2359312 | tf_op jit(solution)/shard_map/reduce_scatter | solution.py:178
  1799.9 5.1 fusion.116
  1805.0 92.0 %reduce-scatter.26.cloned.1.call-done = f32[192,8,192]{2,1,0:T(8,128)} async-done(((f32[1536,8,192]{2,1,0:T(8,128)}), f32[192,8,192]{2,1,0:T(8,128)}) %reduce-scatter.26.cloned.1.call-update) | async-done | bytes 1179664 | tf_op jit(solution)/shard_map/reduce_scatter | solution.py:306
  1897.0 46.3 %reduce-scatter.24.cloned.1.call-done = f32[384,192]{0,1:T(8,128)} async-done(((f32[384,1536]{0,1:T(8,128)}), f32[384,192]{0,1:T(8,128)}) %reduce-scatter.24.cloned.1.call-update) | async-done | bytes 294928 | tf_op jit(solution)/shard_map/reduce_scatter | solution.py:305
  1943.3 46.6 %reduce-scatter.22.cloned.1.call-done = f32[192,384]{1,0:T(8,128)} async-done(((f32[1536,384]{1,0:T(8,128)}), f32[192,384]{1,0:T(8,128)}) %reduce-scatter.22.cloned.1.call-update) | async-done | bytes 294928 | tf_op jit(solution)/shard_map/reduce_scatter | solution.py:304
  1990.0 46.3 %reduce-scatter.20.cloned.1.call-done = f32[192,384]{1,0:T(8,128)} async-done(((f32[1536,384]{1,0:T(8,128)}), f32[192,384]{1,0:T(8,128)}) %reduce-scatter.20.cloned.1.call-update) | async-done | bytes 294928 | tf_op jit(solution)/shard_map/reduce_scatter | solution.py:303
  2036.3 46.8 %reduce-scatter.18.cloned.1.call-done = f32[192,384]{1,0:T(8,128)} async-done(((f32[1536,384]{1,0:T(8,128)}), f32[192,384]{1,0:T(8,128)}) %reduce-scatter.18.cloned.1.call-update) | async-done | bytes 294928 | tf_op jit(solution)/shard_map/reduce_scatter | solution.py:302
  (270 shorter events, 200.9 us)
Async XLA Ops:
  7.2 29.7 %all-gather.18.cloned.1.call-start = ((), (), s32[]{:S(2)}) async-start(), calls=%async_computation.12 | async-start | bytes 1327104 | tf_op jit(solution)/shard_map/all_gather | solution.py:57
  7.9 54.9 %all-gather.16.cloned.1.call-start = ((), (), s32[]{:S(2)}) async-start(), calls=%async_computation.11 | async-start | bytes 1327104 | tf_op jit(solution)/shard_map/all_gather | solution.py:56
  8.7 80.2 %all-gather.14.cloned.1.call-start = ((), (), s32[]{:S(2)}) async-start(), calls=%async_computation.10 | async-start | bytes 1327104 | tf_op jit(solution)/shard_map/all_gather | solution.py:58
  9.4 170.3 %all-gather.12.cloned.1.call-start = ((), (), s32[]{:S(2)}) async-start(), calls=%async_computation.9 | async-start | bytes 5898240 | tf_op jit(solution)/shard_map/all_gather | solution.py:68
  10.0 244.3 %all-gather.20.cloned.1.call-start = ((), (), s32[]{:S(2)}) async-start(), calls=%async_computation.13 | async-start | bytes 1327104 | tf_op jit(solution)/shard_map/all_gather | solution.py:59
  29.3 153.9 %copy-start.25 = (f32[1536]{0:T(1024)}, f32[1536]{0:T(1024)S(1)}, u32[]{:S(2)}) copy-start(f32[1536]{0:T(1024)S(1)} %convert_element_type.148) | copy-start | bytes 18436
  30.5 158.1 %copy-start.14 = (f32[512,64]{0,1:T(8,128)}, f32[512,64]{0,1:T(8,128)S(1)}, u32[]{:S(2)}) copy-start(f32[512,64]{0,1:T(8,128)S(1)} %get-tuple-element.456) | copy-start | bytes 393220
  179.7 3.8 copy-start.2
  184.6 8.8 copy-start.12
  190.4 14.7 collective-permute-start.1
  197.0 10.5 collective-permute-start
  199.4 693.4 %all-gather.30.cloned.1.call-start = ((), (), s32[]{:S(2)}) async-start(), calls=%async_computation.26 | async-start | bytes 47185920 | tf_op jit(solution)/shard_map/all_gather | solution.py:128
  250.4 11.9 copy-start.3
  250.4 11.9 copy-start.20
  250.4 11.9 copy-start.27
  262.4 720.0 %all-gather.26.cloned.1.call-start = ((), (), s32[]{:S(2)}) async-start(), calls=%async_computation.16 | async-start | bytes 5898240 | tf_op jit(solution)/shard_map/all_gather | solution.py:69
  263.1 765.7 %all-gather.24.cloned.1.call-start = ((), (), s32[]{:S(2)}) async-start(), calls=%async_computation.15 | async-start | bytes 7077888 | tf_op jit(solution)/shard_map/all_gather | solution.py:61
  265.0 811.3 %all-gather.22.cloned.1.call-start = ((), (), s32[]{:S(2)}) async-start(), calls=%async_computation.14 | async-start | bytes 7077888 | tf_op jit(solution)/shard_map/all_gather | solution.py:60
  265.7 1086.8 %reduce-scatter.14.cloned.1.call-start = ((), (), s32[]{:S(2)}) async-start(), calls=%async_computation.18 | async-start | bytes 11796480 | tf_op jit(solution)/shard_map/reduce_scatter | solution.py:181
  266.3 656.0 %copy-start.22 = (f32[1536]{0:T(1024)}, f32[1536]{0:T(1024)S(1)}, u32[]{:S(2)}) copy-start(f32[1536]{0:T(1024)S(1)} %convert_element_type.152) | copy-start | bytes 18436
  1089.4 19.6 slice-start
  1098.2 10.8 slice-start.1
  1110.0 11.0 slice-start.10
  1114.8 6.3 slice-start.11
  1148.3 204.2 %copy-start.23 = (f32[1536]{0:T(1024)S(1)}, f32[1536]{0:T(1024)}, u32[]{:S(2)}) copy-start(f32[1536]{0:T(1024)} %copy-done.22) | copy-start | bytes 18436
  1148.4 301.6 %all-gather.28.cloned.1.call-start = ((), (), s32[]{:S(2)}) async-start(), calls=%async_computation.19 | async-start | bytes 5898240 | tf_op jit(solution)/shard_map/all_gather | solution.py:195
  1148.4 207.8 %copy-start.8 = (bf16[3,128,1536]{2,1,0:T(8,128)(2,1)S(1)}, bf16[3,128,1536]{2,1,0:T(8,128)(2,1)}, u32[]{:S(2)}) copy-start(bf16[3,128,1536]{2,1,0:T(8,128)(2,1)} %param.27) | copy-start | bytes 3538948
  1352.6 3.6 copy-start.5
  1359.6 262.8 %reduce-scatter.28.cloned.1.call-start = ((), (), s32[]{:S(2)}) async-start(), calls=%async_computation.27 | async-start | bytes 10616832
  1385.7 64.3 %copy-start.16 = (bf16[384,1536]{0,1:T(8,128)(2,1)S(1)}, bf16[384,1536]{0,1:T(8,128)(2,1)}, u32[]{:S(2)}) copy-start(bf16[384,1536]{0,1:T(8,128)(2,1)} %all-gather.20.cloned.1.call-done) | copy-start | bytes 3538948
  1385.7 293.4 %reduce-scatter.16.cloned.1.call-start = ((), (), s32[]{:S(2)}) async-start(), calls=%async_computation.20 | async-start | bytes 5898240 | tf_op jit(solution)/shard_map/reduce_scatter | solution.py:279
  1454.9 3.7 copy-start.4
  1455.0 3.7 copy-start.21
  1455.0 3.7 copy-start.28
  1511.0 4.7 collective-permute-start.3
  1512.3 6.6 collective-permute-start.2
  1534.7 4.5 copy-start.10
  1550.9 249.0 %reduce-scatter.12.cloned.1.call-start = ((), (), s32[]{:S(2)}) async-start(), calls=%async_computation.17 | async-start | bytes 11796480 | tf_op jit(solution)/shard_map/reduce_scatter | solution.py:178
  1551.5 345.5 %reduce-scatter.26.cloned.1.call-start = ((), (), s32[]{:S(2)}) async-start(), calls=%async_computation.25 | async-start | bytes 14155776 | tf_op jit(solution)/shard_map/reduce_scatter | solution.py:306
  1564.5 378.9 %reduce-scatter.24.cloned.1.call-start = ((), (), s32[]{:S(2)}) async-start(), calls=%async_computation.24 | async-start | bytes 2654208 | tf_op jit(solution)/shard_map/reduce_scatter | solution.py:305
  1571.9 418.1 %reduce-scatter.22.cloned.1.call-start = ((), (), s32[]{:S(2)}) async-start(), calls=%async_computation.23 | async-start | bytes 2654208 | tf_op jit(solution)/shard_map/reduce_scatter | solution.py:304
  1578.4 457.9 %reduce-scatter.20.cloned.1.call-start = ((), (), s32[]{:S(2)}) async-start(), calls=%async_computation.22 | async-start | bytes 2654208 | tf_op jit(solution)/shard_map/reduce_scatter | solution.py:303
  1584.9 498.2 %reduce-scatter.18.cloned.1.call-start = ((), (), s32[]{:S(2)}) async-start(), calls=%async_computation.21 | async-start | bytes 2654208 | tf_op jit(solution)/shard_map/reduce_scatter | solution.py:302
  1622.4 3.7 copy-start.30
  1626.1 53.1 %copy-start.7 = (bf16[3,128,1536]{2,1,0:T(8,128)(2,1)S(1)}, bf16[3,128,1536]{2,1,0:T(8,128)(2,1)}, u32[]{:S(2)}) copy-start(bf16[3,128,1536]{2,1,0:T(8,128)(2,1)} %param.18) | copy-start | bytes 3538948
  1626.1 53.1 %copy-start.26 = (f32[1536]{0:T(1024)S(1)}, f32[1536]{0:T(1024)}, u32[]{:S(2)}) copy-start(f32[1536]{0:T(1024)} %copy-done.25) | copy-start | bytes 18436
  1632.6 167.3 %copy-start.6 = (f32[3,128,1536]{2,1,0:T(8,128)S(1)}, f32[3,128,1536]{2,1,0:T(8,128)}, u32[]{:S(2)}) copy-start(f32[3,128,1536]{2,1,0:T(8,128)} %reduce-scatter.14.cloned.1.call-done) | copy-start | bytes 7077892
  1632.6 167.2 %copy-start.24 = (f32[1536]{0:T(1024)S(1)}, f32[1536]{0:T(1024)}, u32[]{:S(2)}) copy-start(f32[1536]{0:T(1024)} %copy-done.22) | copy-start | bytes 18436
  (17 other events, 30.9 us)
Sparse Core Ops, SparseCore 0:
  9.9 26.9 all-gather.17
  38.8 24.0 all-gather.15
  64.7 24.0 all-gather.13
  90.3 89.3 all-gather.11
  199.5 22.5 all-gather.19
  262.5 630.2 all-gather.29
  894.4 87.9 all-gather.25
  984.8 43.9 all-gather.23
  1030.7 45.5 all-gather.21
  1148.5 204.0 reduce-scatter.13
  1359.7 90.2 all-gather.27
  1453.3 74.9 reduce-scatter.27
  1551.0 84.7 reduce-scatter.15
  1638.0 161.8 reduce-scatter.11
  1803.8 93.1 reduce-scatter.25
  1900.8 42.4 reduce-scatter.23
  1947.5 42.4 reduce-scatter.21
  1993.7 42.4 reduce-scatter.19
  2040.6 42.4 reduce-scatter.17
